TPU v7x, 256 devices: a whole 4x4x8 slice. The times are simulated.
256 devices in a mesh: section: 8 (over x, core), seq: 32 (over z, y).
Axes of the slice: x: 4, y: 4, z: 8, core: 2. Of those that a mesh axis runs over, the one named last changes fastest.
Arguments:
- saved_section_input: bfloat16 [8, 4096, 1024], P('section', 'seq'), may hold values from -6 to 6
- out_cot: bfloat16 [8, 4096, 1024], P('section', 'seq'), may hold values from -6 to 6
- kernel_weight: bfloat16 [8, 2, 3, 64, 16, 32], P('section'), may hold values from -0.875 to 0.875
- blend_weight: bfloat16 [8, 2, 1024, 1024], P('section'), may hold values from -0.1875 to 0.1875
- hazard_head: bfloat16 [1024, 64], replicated, may hold values from -0.75 to 0.75
- labels: int32 [4096], P('seq'), may hold values from 0 to 63
- events: int32 [4096], P('seq'), may hold values 0 or 1
Outputs:
- input_grad: bfloat16 [8, 4096, 1024], P('section', 'seq')
- next_cot: bfloat16 [8, 4096, 1024], P('section', 'seq')
- mix_grad: float32 [8, 1024, 2, 1024], P('section', 'seq')
- conv_grad: float32 [8, 2, 3, 64, 16, 32], P('section', None, None, 'seq')
All inputs are finite; a program needn't handle non-finite values. No bound on the sum of `events` on one device may be relied on, other than what follows from the above.
Results may differ from a plain program's by a relative error of at most 0.006.
Values may be sent and summed in bfloat16 or wider, within the bound.
A program may use at most 64 MiB of HBM per device.

v0:
```python
import jax
import jax.numpy as jnp
from jax import lax
from jax.sharding import PartitionSpec as P

SPAN = 2


exact_mode = lax.Precision.HIGHEST


def from_behind(value, axis, steps):
    count = lax.axis_size(axis)
    leading, last = (max(0, -steps), min(count, count - steps))
    return lax.ppermute(value, axis, [(source, source + steps) for source in range(leading, last)])


def gate_values(preact, group_size):
    filt = preact[..., :group_size].astype(jnp.float32)
    gate_part = preact[..., group_size:].astype(jnp.float32)
    return jnp.tanh(filt) * jax.nn.sigmoid(gate_part)


def gate_grad(preact, dgated, group_size):
    filt = jnp.tanh(preact[..., :group_size].astype(jnp.float32))
    gate_part = jax.nn.sigmoid(preact[..., group_size:].astype(jnp.float32))
    return jnp.concatenate(
        [dgated * gate_part * (1.0 - filt * filt), dgated * filt * gate_part * (1.0 - gate_part)],
        axis=-1,
    )


def layer_forward_pass(tap_list, weight_set, mix_matrix, groups, group_size):
    row_count, channels = tap_list[0].shape
    summed = jnp.zeros((row_count, groups, 2 * group_size), jnp.float32)
    for k in range(3):
        summed = summed + jnp.einsum(
            "rgi,gio->rgo",
            tap_list[k].reshape(row_count, groups, group_size),
            weight_set[k],
            preferred_element_type=jnp.float32,
        )
    preact = summed.astype(jnp.bfloat16)
    gated = gate_values(preact, group_size).reshape(row_count, channels).astype(jnp.bfloat16)
    output = (
        tap_list[0].astype(jnp.float32)
        + jnp.dot(gated, mix_matrix, preferred_element_type=jnp.float32)
    ).astype(jnp.bfloat16)
    return (preact, gated, output)


def transpose_tap(dpre, weight_set, k):
    return jnp.einsum("rgo,gio->rgi", dpre, weight_set[k].astype(jnp.float32), precision=exact_mode)


def weight_terms(tap_list, dpre, groups, group_size):
    row_count = dpre.shape[0]
    return jnp.stack(
        [
            jnp.einsum(
                "rgi,rgo->gio",
                tap.reshape(row_count, groups, group_size).astype(jnp.float32),
                dpre,
                precision=exact_mode,
            )
            for tap in tap_list
        ]
    )


def body(saved_section_input, out_cot, kernel_weight, blend_weight, hazard_head, labels, events):
    first_input = saved_section_input[0]
    row_count, channels = first_input.shape
    weights = kernel_weight[0]
    mixes = blend_weight[0]
    groups = weights.shape[2]
    group_size = weights.shape[3]
    short_reach = row_count // 8
    edge_rows = from_behind(first_input[row_count - 2 * short_reach :], "seq", 1)
    extended = jnp.concatenate([edge_rows, first_input], axis=0)
    taps_short = [
        extended[2 * short_reach - k * short_reach : 2 * short_reach - k * short_reach + row_count]
        for k in range(3)
    ]
    pre_short, gated_short, middle = layer_forward_pass(
        taps_short, weights[0], mixes[0], groups, group_size
    )
    near_rows = from_behind(middle, "seq", SPAN)
    far_rows = from_behind(middle, "seq", 2 * SPAN)
    taps_long = [middle, near_rows, far_rows]
    pre_long, gated_long, top = layer_forward_pass(
        taps_long, weights[1], mixes[1], groups, group_size
    )
    section_index = lax.axis_index("section")
    is_last = section_index == lax.axis_size("section") - 1
    logits = jnp.dot(top, hazard_head, preferred_element_type=jnp.float32)
    hazard = jax.nn.sigmoid(logits)
    bin_ids = lax.broadcasted_iota(jnp.int32, logits.shape, 1)
    below = (bin_ids <= labels[:, None]).astype(jnp.float32)
    at_label = (bin_ids == labels[:, None]).astype(jnp.float32) * events[:, None].astype(
        jnp.float32
    )
    dlogit = (hazard * below - at_label).astype(jnp.bfloat16)
    loss_cot = jnp.dot(dlogit, hazard_head.T, preferred_element_type=jnp.float32)
    upstream_gradient = (out_cot[0].astype(jnp.float32) + jnp.where(is_last, loss_cot, 0.0)).astype(
        jnp.bfloat16
    )
    dgated_long = jnp.dot(
        upstream_gradient, mixes[1].T, preferred_element_type=jnp.float32
    ).reshape(row_count, groups, group_size)
    dpre_long = gate_grad(pre_long, dgated_long, group_size)
    near_cot = from_behind(dpre_long, "seq", -SPAN)
    far_cot = from_behind(dpre_long, "seq", -2 * SPAN)
    convolution_wide = (
        transpose_tap(dpre_long, weights[1], 0)
        + transpose_tap(near_cot, weights[1], 1)
        + transpose_tap(far_cot, weights[1], 2)
    )
    between_gradient = (
        upstream_gradient.astype(jnp.float32) + convolution_wide.reshape(row_count, channels)
    ).astype(jnp.bfloat16)
    dgated_short = jnp.dot(
        between_gradient, mixes[0].T, preferred_element_type=jnp.float32
    ).reshape(row_count, groups, group_size)
    dpre_short = gate_grad(pre_short, dgated_short, group_size)
    next_rows = from_behind(dpre_short[: 2 * short_reach].astype(jnp.bfloat16), "seq", -1).astype(
        jnp.float32
    )
    extended_back = jnp.concatenate([dpre_short, next_rows], axis=0)
    convolution_narrow = transpose_tap(dpre_short, weights[0], 0)
    for k in range(1, 3):
        convolution_narrow = convolution_narrow + transpose_tap(
            extended_back[k * short_reach : k * short_reach + row_count], weights[0], k
        )
    input_gradient_rows = (
        between_gradient.astype(jnp.float32) + convolution_narrow.reshape(row_count, channels)
    ).astype(jnp.bfloat16)
    received = from_behind(input_gradient_rows, "section", -1)
    next_cot = jnp.where(is_last, upstream_gradient, received)
    mix_share = lax.psum_scatter(
        jnp.stack(
            [
                jnp.dot(gated_short.T, between_gradient, preferred_element_type=jnp.float32),
                jnp.dot(gated_long.T, upstream_gradient, preferred_element_type=jnp.float32),
            ],
            axis=1,
        ),
        "seq",
        scatter_dimension=0,
        tiled=True,
    )
    conv_terms = jnp.stack(
        [
            weight_terms(taps_short, dpre_short, groups, group_size),
            weight_terms(taps_long, dpre_long, groups, group_size),
        ]
    )
    conv_share = lax.psum_scatter(conv_terms, "seq", scatter_dimension=2, tiled=True)
    return (input_gradient_rows[None], next_cot[None], mix_share[None], conv_share[None])


def solution(mesh):
    return jax.shard_map(
        body,
        mesh=mesh,
        in_specs=(
            P("section", "seq", None),
            P("section", "seq", None),
            P("section", None, None, None, None, None),
            P("section", None, None, None),
            P(),
            P("seq"),
            P("seq"),
        ),
        out_specs=(
            P("section", "seq", None),
            P("section", "seq", None),
            P("section", "seq", None, None),
            P("section", None, None, "seq", None, None),
        ),
        check_vma=False,
    )
```

profile of v0, /device:TPU:14, one launch (start us, length us, event | category | flops | bytes accessed | tf_op | source)
XLA Modules:
  0.0 507.3 jit_solution(9016351092181387672)
XLA Ops:
  8.1 3.6 collective-permute-start
  11.7 4.7 fusion.79
  20.6 1.2 fusion.7
  21.8 1.2 multiply_convert_fusion.1
  23.0 1.2 fusion.20
  24.2 1.1 copy.61
  25.4 4.5 collective-permute-start.2
  29.9 4.2 collective-permute-start.1
  34.5 4.9 collective-permute-done.1
  40.0 1.1 copy.65
  41.1 1.3 fusion.8
  43.2 2.3 fusion.44
  45.8 2.4 subtract_multiply_fusion.3
  48.4 1.3 collective-permute-start.3
  49.7 1.5 collective-permute-start.4
  51.1 1.7 convolution_bitcast_fusion.7
  52.9 1.7 convolution_bitcast_fusion.6
  54.6 1.7 convolution_bitcast_fusion.5
  56.9 18.9 %collective-permute-done.3 = f32[128,64,32]{0,2,1:T(8,128)S(1)} collective-permute-done((f32[128,64,32]{0,2,1:T(8,128)S(1)}, f32[128,64,32]{0,2,1:T(8,128)S(1)}, u32[]{:S(2)}, u32[]{:S(2)}) %collective-permute-start.3) | collective-permute-done | bytes 1048608 | tf_op jit(solution)/shard_map/ppermute | solution.py:15
  76.4 23.5 %collective-permute-done.4 = f32[128,64,32]{0,2,1:T(8,128)S(1)} collective-permute-done((f32[128,64,32]{0,2,1:T(8,128)S(1)}, f32[128,64,32]{0,2,1:T(8,128)S(1)}, u32[]{:S(2)}, u32[]{:S(2)}) %collective-permute-start.4) | collective-permute-done | bytes 1048608 | tf_op jit(solution)/shard_map/ppermute | solution.py:15
  100.9 2.4 subtract_multiply_fusion.1
  105.2 0.9 convolution_bitcast_fusion.10
  106.5 2.0 pad_maximum_fusion.1
  110.9 4.1 pad_maximum_fusion
  115.1 3.0 collective-permute-start.5
  118.8 16.7 %collective-permute-done.5 = bf16[32,64,32]{0,2,1:T(8,128)(2,1)S(1)} collective-permute-done((bf16[32,64,32]{0,2,1:T(8,128)(2,1)S(1)}, bf16[32,64,32]{0,2,1:T(8,128)(2,1)S(1)}, u32[]{:S(2)}, u32[]{:S(2)}) %collective-permute-start.5) | collective-permute-done | bytes 131104 | tf_op jit(solution)/shard_map/ppermute | solution.py:15
  137.8 1.9 collective-permute-start.6
  141.0 2.6 collective-permute-done.6
  144.3 123.5 %all-reduce.3.cloned.1.call-done = f32[2,3,64,16,32]{4,3,2,1,0:T(8,128)} async-done(((f32[2,3,64,16,32]{4,3,2,1,0:T(8,128)}), f32[2,3,64,16,32]{4,3,2,1,0:T(8,128)}) %all-reduce.3.cloned.1.call-update) | async-done | bytes 786448
  267.8 1.5 dynamic-slice_bitcast_fusion
  269.3 229.2 %reduce-scatter.5.cloned.1.call-done = f32[32,2,1024]{2,0,1:T(8,128)} async-done(((f32[1024,2,1024]{2,0,1:T(8,128)}), f32[32,2,1024]{2,0,1:T(8,128)}) %reduce-scatter.5.cloned.1.call-update) | async-done | bytes 262160 | tf_op jit(solution)/shard_map/reduce_scatter | solution.py:140
  498.6 1.9 copy.75
  (103 shorter events, 17.9 us)
Async XLA Ops:
  7.2 36.1 %copy-start = (bf16[1024,64]{0,1:T(8,128)(2,1)S(1)}, bf16[1024,64]{0,1:T(8,128)(2,1)}, u32[]{:S(2)}) copy-start(bf16[1024,64]{0,1:T(8,128)(2,1)} %param.11) | copy-start | bytes 393220
  7.2 260.6 %all-reduce.3.cloned.1.call-start = ((), (), s32[]{:S(2)}) async-start(), calls=%async_computation.2 | async-start | bytes 6291456
  8.1 8.4 %copy-start.22 = (bf16[1,2,3,64,16,32]{3,5,4,2,1,0:T(8,128)(2,1)S(1)}, bf16[1,2,3,64,16,32]{3,5,4,2,1,0:T(8,128)(2,1)}, u32[]{:S(2)}) copy-start(bf16[1,2,3,64,16,32]{3,5,4,2,1,0:T(8,128)(2,1)} %param.9) | copy-start | bytes 1179652
  8.1 8.4 %copy-start.2 = (bf16[1,128,1024]{2,1,0:T(8,128)(2,1)S(1)}, bf16[1,128,1024]{2,1,0:T(8,128)(2,1)}, u32[]{:S(2)}) copy-start(bf16[1,128,1024]{2,1,0:T(8,128)(2,1)} %param.7) | copy-start | bytes 786436
  8.1 11.3 %collective-permute-start = (bf16[32,1024]{1,0:T(8,128)(2,1)S(1)}, bf16[32,1024]{1,0:T(8,128)(2,1)S(1)}, u32[]{:S(2)}, u32[]{:S(2)}) collective-permute-start(bf16[32,1024]{1,0:T(8,128)(2,1)S(1)} %slice_bitcast_fusion), channel_id=1, source_target_pairs={{0,1},{1,2},{2,3},{3,4},{4,5},{5,6},{6,7},{7,8},{8,9},{9,10},{10,1... | collective-permute-start | bytes 196616 | tf_op jit(solution)/shard_map/ppermute | solution.py:15
  18.6 15.5 %copy-start.5 = (bf16[1,1,1,64,16,32]{5,4,3,2,1,0:T(8,128)(2,1)}, bf16[1,1,1,64,16,32]{5,4,3,2,1,0:T(8,128)(2,1)S(1)}, u32[]{:S(2)}) copy-start(bf16[1,1,1,64,16,32]{5,4,3,2,1,0:T(8,128)(2,1)S(1)} %copy.85) | copy-start | bytes 196612
  18.8 1.7 copy-start.11
  19.6 1.0 copy-start.14
  20.2 2.8 copy-start.1
  23.0 11.5 %copy-start.9 = (bf16[128,64,16]{0,2,1:T(8,128)(2,1)}, bf16[128,64,16]{0,2,1:T(8,128)(2,1)S(1)}, u32[]{:S(2)}) copy-start(bf16[128,64,16]{0,2,1:T(8,128)(2,1)S(1)} %multiply_convert_fusion.1) | copy-start | bytes 786436
  25.3 14.2 %copy-start.7 = (bf16[128,1024]{0,1:T(8,128)(2,1)}, bf16[128,1024]{0,1:T(8,128)(2,1)S(1)}, u32[]{:S(2)}) copy-start(bf16[128,1024]{0,1:T(8,128)(2,1)S(1)} %copy.61) | copy-start | bytes 786436
  25.4 14.6 %collective-permute-start.2 = (bf16[128,1024]{1,0:T(8,128)(2,1)}, bf16[128,1024]{1,0:T(8,128)(2,1)}, u32[]{:S(2)}, u32[]{:S(2)}) collective-permute-start(bf16[128,1024]{1,0:T(8,128)(2,1)} %fusion.20), channel_id=1, source_target_pairs={{0,4},{1,5},{2,6},{3,7},{4,8},{5,9},{6,10},{7,11},{8,12},{9,13},{1... | collective-permute-start | bytes 786440 | tf_op jit(solution)/shard_map/ppermute | solution.py:15
  29.9 9.5 %collective-permute-start.1 = (bf16[128,1024]{1,0:T(8,128)(2,1)}, bf16[128,1024]{1,0:T(8,128)(2,1)S(1)}, u32[]{:S(2)}, u32[]{:S(2)}) collective-permute-start(bf16[128,1024]{1,0:T(8,128)(2,1)} %fusion.20), channel_id=1, source_target_pairs={{0,2},{1,3},{2,4},{3,5},{4,6},{5,7},{6,8},{7,9},{8,10},{9,11},{10,... | collective-permute-start | bytes 786440 | tf_op jit(solution)/shard_map/ppermute | solution.py:15
  39.9 3.3 copy-start.26
  42.4 3.1 copy-start.23
  42.6 5.5 %copy-start.20 = (bf16[128,64,16]{0,2,1:T(8,128)(2,1)}, bf16[128,64,16]{0,2,1:T(8,128)(2,1)S(1)}, u32[]{:S(2)}) copy-start(bf16[128,64,16]{0,2,1:T(8,128)(2,1)S(1)} %multiply_convert_fusion) | copy-start | bytes 786436
  48.2 2.9 copy-start.8
  48.4 27.5 %collective-permute-start.3 = (f32[128,64,32]{0,2,1:T(8,128)S(1)}, f32[128,64,32]{0,2,1:T(8,128)S(1)}, u32[]{:S(2)}, u32[]{:S(2)}) collective-permute-start(f32[128,64,32]{0,2,1:T(8,128)S(1)} %pad_maximum_fusion.4), channel_id=1, source_target_pairs={{2,0},{3,1},{4,2},{5,3},{6,4},{7,5},{8,6},{9,7},{10,8},{11,9},{12,... | collective-permute-start | bytes 3145736 | tf_op jit(solution)/shard_map/ppermute | solution.py:15
  49.7 50.3 %collective-permute-start.4 = (f32[128,64,32]{0,2,1:T(8,128)S(1)}, f32[128,64,32]{0,2,1:T(8,128)S(1)}, u32[]{:S(2)}, u32[]{:S(2)}) collective-permute-start(f32[128,64,32]{0,2,1:T(8,128)S(1)} %pad_maximum_fusion.4), channel_id=1, source_target_pairs={{4,0},{5,1},{6,2},{7,3},{8,4},{9,5},{10,6},{11,7},{12,8},{13,9},{1... | collective-permute-start | bytes 3145736 | tf_op jit(solution)/shard_map/ppermute | solution.py:15
  52.9 3.5 copy-start.6
  56.3 43.6 %copy-start.13 = (bf16[1,1,1,64,16,32]{5,4,3,2,1,0:T(8,128)(2,1)S(1)}, bf16[1,1,1,64,16,32]{5,4,3,2,1,0:T(8,128)(2,1)}, u32[]{:S(2)}) copy-start(bf16[1,1,1,64,16,32]{5,4,3,2,1,0:T(8,128)(2,1)} %copy.87) | copy-start | bytes 196612
  100.8 2.5 copy-start.4
  100.8 3.4 copy-start.15
  104.2 1.9 copy-start.16
  104.3 1.9 copy-start.17
  104.3 1.9 copy-start.18
  108.6 1.6 copy-start.10
  108.6 390.0 %reduce-scatter.5.cloned.1.call-start = ((), (), s32[]{:S(2)}) async-start(), calls=%async_computation.1 | async-start | bytes 8650752 | tf_op jit(solution)/shard_map/reduce_scatter | solution.py:140
  115.1 20.3 %collective-permute-start.5 = (bf16[32,64,32]{0,2,1:T(8,128)(2,1)S(1)}, bf16[32,64,32]{0,2,1:T(8,128)(2,1)S(1)}, u32[]{:S(2)}, u32[]{:S(2)}) collective-permute-start(bf16[32,64,32]{0,2,1:T(8,128)(2,1)S(1)} %fusion.48), channel_id=1, source_target_pairs={{1,0},{2,1},{3,2},{4,3},{5,4},{6,5},{7,6},{8,7},{9,8},{10,9},{11,1... | collective-permute-start | bytes 393224 | tf_op jit(solution)/shard_map/ppermute | solution.py:15
  136.8 3.0 copy-start.27
  137.8 362.6 %copy-start.24 = (bf16[128,1024]{1,0:T(8,128)(2,1)}, bf16[128,1024]{1,0:T(8,128)(2,1)S(1)}, u32[]{:S(2)}) copy-start(bf16[128,1024]{1,0:T(8,128)(2,1)S(1)} %add_convert_fusion) | copy-start | bytes 786436
  137.8 5.8 %collective-permute-start.6 = (bf16[128,1024]{1,0:T(8,128)(2,1)S(1)}, bf16[128,1024]{1,0:T(8,128)(2,1)S(1)}, u32[]{:S(2)}, u32[]{:S(2)}) collective-permute-start(bf16[128,1024]{1,0:T(8,128)(2,1)S(1)} %add_convert_fusion), channel_id=1, source_target_pairs={{32,0},{64,32},{96,64},{128,96},{160,128},{192,160},{224,192},{33,... | collective-permute-start | bytes 786440 | tf_op jit(solution)/shard_map/ppermute | solution.py:15
  (5 other events, 4.1 us)
Sparse Core Ops, SparseCore 0:
  108.7 159.0 all-reduce.2
  272.3 226.1 reduce-scatter.4
where the time goes:
time: 509 us; the launch traced here: 507 us
  waiting for transfers between devices  419 us (82%)
  matrix products  25.8 us (5%)
  starting transfers between devices  20.2 us (4%)
  local copies, waits for them, and re-layouts  17.3 us (3%)
  between operations  15.4 us (3%)
  other arithmetic  9.39 us (2%)
    reduce_scatter x1, waiting for transfers between devices, body(): lax.psum_scatter(jnp.stack([jnp.dot(gated_short.T, between_gradient, pref...  229 us
    unnamed x3, waiting for transfers between devices  124 us
    ppermute x7, waiting for transfers between devices, from_behind(): lax.ppermute(value, axis, [(source, source + steps) for source in range(l...  66.6 us
    ppermute x7, starting transfers between devices, from_behind(): lax.ppermute(value, axis, [(source, source + steps) for source in range(l...  20.1 us
  transfers between devices with their start and end apart: 9, of which 7 were waited for; matrix products, arithmetic and copies ran while one was open for 5% of the time, Pallas kernels for 0%

commit v1 on v0

v1 whole, which is shorter than its diff:
```python
import functools

import jax
import jax.numpy as jnp
from jax import lax
from jax.experimental import pallas as pl
from jax.experimental.pallas import tpu as pltpu
from jax.sharding import PartitionSpec as P

MESH = pl.DeviceIdType.MESH
F32 = jnp.float32
BF = jnp.bfloat16
NY = 4
LANE = 128

NT = (((1,), (1,)), ((), ()))
TN = (((0,), (0,)), ((), ()))
NN = (((1,), (0,)), ((), ()))


def mm(a, b, dims):
    return lax.dot_general(a, b, dims, preferred_element_type=F32)


def iota(shape, dim):
    return lax.broadcasted_iota(jnp.int32, shape, dim)


def out_channel(col):
    return jnp.where(col < LANE, col & 15, 16 + (col & 15))


def expand_weights(kw, layer, wbd, groups):
    half = groups * 16 // 2
    sel = jnp.where(
        out_channel(iota((512, 256), 1)) == (iota((512, 256), 0) & 31), 1.0, 0.0
    ).astype(BF)
    keep_in = (iota((half, 512), 1) >> 5) == (iota((half, 512), 0) & 15)
    keep_group = ((iota((half, 256), 0) >> 4) & 7) == ((iota((half, 256), 1) & 127) >> 4)
    for part in range(2):
        pick = jnp.where(
            (iota((half, groups), 0) >> 4) + part * (groups // 2) == iota((half, groups), 1),
            1.0,
            0.0,
        ).astype(BF)
        for k in range(3):
            rows = mm(pick, kw[3 * layer + k], NT)
            rows = jnp.where(keep_in, rows, 0.0).astype(BF)
            full = jnp.where(keep_group, mm(rows, sel, NN), 0.0).astype(BF)
            for b in range(half // LANE):
                wbd[part * (half // LANE) + b, k * LANE : (k + 1) * LANE, :] = full[
                    b * LANE : (b + 1) * LANE
                ]


def kernel(nz, nsec, *refs):
    (x_in, cot_in, kw_in, mix_in, head_in, lab_in, ev_in) = refs[:7]
    (ig_out, nc_out, mg_out, cg_out) = refs[7:11]
    (ext, g, kw, mix, head, lab, ev, wbd, gated, fac, mid, near, far, dpre, acc, snd_n, snd_f,
     rcv_n, rcv_f, btw, tap1, tap2, hal_s, hal_r, nxt, part, fin, lsem, ssem, rsem) = refs[11:41]
    pools = refs[41:]

    rows, chans = mid.shape
    nq = NY * nz
    rd = chans // nq
    blocks = chans // LANE
    groups = chans // 16
    width = part.shape[-1]
    sec = lax.axis_index("section")
    q = lax.axis_index("seq")
    y = lax.rem(q, NY)
    z = q // NY
    last = sec == nsec - 1

    def seq(step):
        return {"seq": lax.rem(q + step + nq, nq)}

    def ydev(step):
        return {"seq": z * NY + lax.rem(y + step + NY, NY)}

    def zdev(step):
        return {"seq": lax.rem(z + step + nz, nz) * NY + y}

    loads = []
    for i, (src, dst) in enumerate(
        [
            (x_in.at[0], ext.at[pl.ds(32, rows)]),
            (kw_in, kw),
            (mix_in.at[0, 0], mix.at[0]),
            (cot_in.at[0], g),
            (mix_in.at[0, 1], mix.at[1]),
            (head_in, head),
            (lab_in, lab),
            (ev_in, ev),
        ]
    ):
        copy = pltpu.make_async_copy(src, dst, lsem.at[i])
        copy.start()
        loads.append(copy)

    count = [0]

    def push(src, dst, target):
        n = count[0]
        count[0] += 1
        copy = pltpu.make_async_remote_copy(
            src_ref=src,
            dst_ref=dst,
            send_sem=ssem.at[n],
            recv_sem=rsem.at[n],
            device_id=target,
            device_id_type=MESH,
        )
        copy.start()
        return copy

    barrier = pltpu.get_barrier_semaphore()
    greet = [seq(1), seq(-1), seq(2), seq(-2), seq(NY), seq(-NY), ydev(1), ydev(-1)]
    greet.append({"section": lax.rem(sec + 1, nsec)})
    for target in greet:
        pl.semaphore_signal(barrier, inc=1, device_id=target, device_id_type=MESH)
    pl.semaphore_wait(barrier, len(greet))

    sends = []
    halo = push(x_in.at[0, pl.ds(rows - 32, 32)], ext.at[pl.ds(0, 32)], seq(1))
    sends.append(halo)

    loads[1].wait()
    expand_weights(kw, 0, wbd.at[0], groups)
    loads[0].wait()
    loads[2].wait()
    halo.wait_recv()

    @pl.when(q == 0)
    def _():
        ext[0:32] = jnp.zeros((32, chans), BF)

    def lanes(b):
        return slice(b * LANE, (b + 1) * LANE)

    def taps_short(b):
        return jnp.concatenate(
            [ext[32 : 32 + rows, lanes(b)], ext[16 : 16 + rows, lanes(b)], ext[0:rows, lanes(b)]],
            axis=1,
        )

    def taps_long(b):
        return jnp.concatenate([mid[:, lanes(b)], near[:, lanes(b)], far[:, lanes(b)]], axis=1)

    def gates(layer, taps):
        for b in range(blocks):
            pre = mm(taps(b), wbd[layer, b], NN).astype(BF).astype(F32)
            filt = jnp.tanh(pre[:, :LANE])
            gate = jax.nn.sigmoid(pre[:, LANE:])
            gated[layer, :, lanes(b)] = (filt * gate).astype(BF)
            fac[layer, 0, :, lanes(b)] = gate * (1.0 - filt * filt)
            fac[layer, 1, :, lanes(b)] = filt * gate * (1.0 - gate)

    gates(0, taps_short)
    mid[...] = (ext[32 : 32 + rows].astype(F32) + mm(gated[0], mix[0], NN)).astype(BF)
    to_near = push(mid, near, seq(2))
    to_far = push(mid, far, seq(NY))
    sends += [to_near, to_far]

    expand_weights(kw, 1, wbd.at[1], groups)
    for copy in loads[3:]:
        copy.wait()
    to_near.wait_recv()
    to_far.wait_recv()

    @pl.when(q < 2)
    def _():
        near[...] = jnp.zeros((rows, chans), BF)

    @pl.when(q < NY)
    def _():
        far[...] = jnp.zeros((rows, chans), BF)

    gates(1, taps_long)

    @pl.when(last)
    def _():
        top = (mid[...].astype(F32) + mm(gated[1], mix[1], NN)).astype(BF)
        hazard = jax.nn.sigmoid(mm(head[...], top, NT))
        bins = iota(hazard.shape, 0)
        below = jnp.where(bins <= lab[...], hazard, 0.0)
        at_label = jnp.where(bins == lab[...], ev[...].astype(F32), 0.0)
        dlogit = (below - at_label).astype(BF)
        g[...] = (g[...].astype(F32) + mm(dlogit, head[...], TN)).astype(BF)

    def cot_of_pre(layer, upstream):
        dgated = mm(upstream, mix[layer], NT)
        for b in range(blocks):
            both = jnp.concatenate(
                [
                    dgated[:, lanes(b)] * fac[layer, 0, :, lanes(b)],
                    dgated[:, lanes(b)] * fac[layer, 1, :, lanes(b)],
                ],
                axis=1,
            ).astype(BF)
            dpre[layer, :, 256 * b : 256 * (b + 1)] = both

    def back_taps(layer, b):
        return mm(dpre[layer, :, 256 * b : 256 * (b + 1)], wbd[layer, b], NT)

    cot_of_pre(1, g[...])
    for b in range(blocks):
        prods = back_taps(1, b)
        acc[:, lanes(b)] = prods[:, :LANE]
        snd_n[:, lanes(b)] = prods[:, LANE : 2 * LANE].astype(BF)
        snd_f[:, lanes(b)] = prods[:, 2 * LANE :].astype(BF)
    back_near = push(snd_n, rcv_n, seq(-2))
    back_far = push(snd_f, rcv_f, seq(-NY))
    sends += [back_near, back_far]

    compact = jnp.where(
        iota((768, LANE), 1) == 32 * (iota((768, LANE), 0) >> 8) + out_channel(iota((768, LANE), 0) & 255),
        1.0,
        0.0,
    ).astype(BF)
    own_group = (iota((LANE, 256), 0) >> 4) == ((iota((LANE, 256), 1) & 127) >> 4)
    per_z = NY * rd

    def weight_terms(layer, taps, upstream):
        for d in range(nz):
            block = mm(gated[layer, :, d * per_z : (d + 1) * per_z], upstream, TN)
            part[layer, d * NY : (d + 1) * NY, :, 0:chans] = block.reshape(NY, rd, chans)
        for b in range(blocks):
            full = mm(taps(b), dpre[layer, :, 256 * b : 256 * (b + 1)], TN)
            kept = jnp.concatenate(
                [
                    jnp.where(own_group, full[k * LANE : (k + 1) * LANE], 0.0).astype(BF)
                    for k in range(3)
                ],
                axis=1,
            )
            packed = mm(kept, compact, NN)
            n = LANE // rd
            part[layer, b * n : (b + 1) * n, :, chans:width] = packed.reshape(n, rd, LANE)

    weight_terms(1, taps_long, g[...])

    back_near.wait_recv()
    back_far.wait_recv()

    @pl.when(q >= nq - 2)
    def _():
        rcv_n[...] = jnp.zeros((rows, chans), BF)

    @pl.when(q >= nq - NY)
    def _():
        rcv_f[...] = jnp.zeros((rows, chans), BF)

    btw[...] = (
        g[...].astype(F32) + acc[...] + rcv_n[...].astype(F32) + rcv_f[...].astype(F32)
    ).astype(BF)
    cot_of_pre(0, btw[...])
    for b in range(blocks):
        prods = back_taps(0, b)
        acc[:, lanes(b)] = prods[:, :LANE]
        tap1[0:rows, lanes(b)] = prods[:, LANE : 2 * LANE]
        tap2[0:rows, lanes(b)] = prods[:, 2 * LANE :]
    hal_s[0:16] = tap2[0:16].astype(BF)
    hal_s[16:32] = (tap1[0:16] + tap2[16:32]).astype(BF)
    back_halo = push(hal_s, hal_r, seq(-1))
    sends.append(back_halo)
    weight_terms(0, taps_short, btw[...])
    tap1[rows : rows + 16] = jnp.zeros((16, chans), F32)
    tap2[rows : rows + 32] = jnp.zeros((32, chans), F32)
    back_halo.wait_recv()

    @pl.when(q == nq - 1)
    def _():
        hal_r[...] = jnp.zeros((32, chans), BF)

    total = btw[...].astype(F32) + acc[...] + tap1[16 : 16 + rows] + tap2[32 : 32 + rows]
    ig_out[0, 0 : rows - 32] = total[0 : rows - 32].astype(BF)
    ig_out[0, rows - 32 : rows] = (total[rows - 32 :] + hal_r[...].astype(F32)).astype(BF)
    to_prev = push(ig_out.at[0], nxt, {"section": lax.rem(sec + nsec - 1, nsec)})
    sends.append(to_prev)

    def ring(n, pos, dev, own, depth, bufs, done):
        right_s, right_r, left_s, left_r = bufs
        half = depth // 2
        arrived = None
        at = 0
        for t in range(1, n // 2 + 1):
            dist = n // 2 - t + 1
            to_r, to_l = lax.rem(pos + dist, n), lax.rem(pos - dist + n, n)
            size = half if t == 1 else depth
            if arrived is not None:
                was, copies = arrived
                for c in copies:
                    c.wait_recv()
            for d in range(depth):
                if t > 1 or d < half:
                    v = own(to_r, d)
                    if t > 2 or (t == 2 and d < half):
                        v = v + right_r[was + d].astype(F32)
                    right_s[at + d] = v.astype(BF)
                if t > 1 or d >= half:
                    v = own(to_l, d)
                    if t > 2 or (t == 2 and d >= half):
                        v = v + left_r[was + (d - half if t == 2 else d)].astype(F32)
                    left_s[at + (d - half if t == 1 else d)] = v.astype(BF)
            copies = [
                push(right_s.at[pl.ds(at, size)], right_r.at[pl.ds(at, size)], dev(1)),
                push(left_s.at[pl.ds(at, size)], left_r.at[pl.ds(at, size)], dev(-1)),
            ]
            sends.extend(copies)
            arrived = (at, copies)
            at += size
            yield
        was, copies = arrived
        for c in copies:
            c.wait_recv()
        for d in range(depth):
            v = own(pos, d)
            if n > 2:
                v = v + right_r[was + d].astype(F32) + left_r[was + d].astype(F32)
            elif d < half:
                v = v + right_r[was + d].astype(F32)
            else:
                v = v + left_r[was + d - half].astype(F32)
            done(d, v)

    def stream(layer, lo, w, y_first, bufs):
        span = slice(lo, lo + w)
        first, mids, second = bufs[0:4], bufs[4], bufs[5:9]
        h = rd // 2

        def keep(d, v):
            mids[d] = v

        def own2(dest, d):
            return mids[dest, d * h : (d + 1) * h, :]

        def finish(d, v):
            fin[layer, d * h : (d + 1) * h, span] = v

        if y_first:
            yield from ring(NY, y, ydev, lambda e, d: part[layer, d * NY + e, :, span], nz, first, keep)
            yield from ring(nz, z, zdev, own2, 2, second, finish)
        else:
            yield from ring(nz, z, zdev, lambda e, d: part[layer, e * NY + d, :, span], NY, first, keep)
            yield from ring(NY, y, ydev, own2, 2, second, finish)

    live = [
        stream(1, 0, width, True, pools[0:9]),
        stream(0, 0, width, False, pools[9:18]),
    ]
    while live:
        for s in list(live):
            try:
                next(s)
            except StopIteration:
                live.remove(s)

    for layer in range(2):
        mg_out[0, :, layer, :] = fin[layer, :, 0:chans]
        for k in range(3):
            cg_out[0, layer, k] = fin[layer, :, chans + 32 * k : chans + 32 * (k + 1)].reshape(
                rd // 16, 16, 32
            )

    to_prev.wait_recv()

    @pl.when(last)
    def _():
        nc_out[0] = g[...]

    @pl.when(jnp.logical_not(last))
    def _():
        nc_out[0] = nxt[...]

    for copy in sends:
        copy.wait_send()


def ring_pool(n, depth, r, w):
    units = depth // 2 + depth * (n // 2 - 1)
    return [pltpu.VMEM((units, r, w), BF)] * 4


def stream_pool(nz, rd, w, y_first):
    n1, n2 = (NY, nz) if y_first else (nz, NY)
    return ring_pool(n1, n2, rd, w) + [pltpu.VMEM((n2, rd, w), F32)] + ring_pool(n2, 2, rd // 2, w)


def solution(mesh):
    nsec, nq = mesh.shape["section"], mesh.shape["seq"]
    nz = nq // NY

    def body(x, cot, kernel_weight, blend, head, labels, events):
        _, rows, chans = x.shape
        groups, gin, gout = kernel_weight.shape[3:]
        rd = chans // nq
        width = chans + LANE
        blocks = chans // LANE
        kw = jnp.transpose(kernel_weight[0], (0, 1, 3, 4, 2)).reshape(6, gin * gout, groups)
        any_ = pl.BlockSpec(memory_space=pl.ANY)
        vm = pl.BlockSpec(memory_space=pltpu.VMEM)
        act = pltpu.VMEM((rows, chans), BF)
        n_push = 8 + 2 * 2 * (NY // 2 + nz // 2)
        scratch = [
            pltpu.VMEM((rows + 32, chans), BF),
            act,
            pltpu.VMEM((6, gin * gout, groups), BF),
            pltpu.VMEM((2, chans, chans), BF),
            pltpu.VMEM((head.shape[1], chans), BF),
            pltpu.VMEM((1, rows), jnp.int32),
            pltpu.VMEM((1, rows), jnp.int32),
            pltpu.VMEM((2, blocks, 3 * LANE, 2 * LANE), BF),
            pltpu.VMEM((2, rows, chans), BF),
            pltpu.VMEM((2, 2, rows, chans), F32),
            act,
            act,
            act,
            pltpu.VMEM((2, rows, 2 * chans), BF),
            pltpu.VMEM((rows, chans), F32),
            act,
            act,
            act,
            act,
            act,
            pltpu.VMEM((rows + 16, chans), F32),
            pltpu.VMEM((rows + 32, chans), F32),
            pltpu.VMEM((32, chans), BF),
            pltpu.VMEM((32, chans), BF),
            act,
            pltpu.VMEM((2, nq, rd, width), F32),
            pltpu.VMEM((2, rd, width), F32),
            pltpu.SemaphoreType.DMA((8,)),
            pltpu.SemaphoreType.DMA((n_push,)),
            pltpu.SemaphoreType.DMA((n_push,)),
        ]
        scratch += stream_pool(nz, rd, width, True) + stream_pool(nz, rd, width, False)
        return pl.pallas_call(
            functools.partial(kernel, nz, nsec),
            out_shape=(
                jax.ShapeDtypeStruct((1, rows, chans), BF),
                jax.ShapeDtypeStruct((1, rows, chans), BF),
                jax.ShapeDtypeStruct((1, rd, 2, chans), F32),
                jax.ShapeDtypeStruct((1, 2, 3, groups // nq, gin, gout), F32),
            ),
            in_specs=[any_] * 7,
            out_specs=(vm, vm, vm, vm),
            scratch_shapes=scratch,
            compiler_params=pltpu.CompilerParams(
                collective_id=0, has_side_effects=True, vmem_limit_bytes=58 * 1024 * 1024
            ),
        )(x, cot, kw, blend, head.T, labels.reshape(1, rows), events.reshape(1, rows))

    return jax.shard_map(
        body,
        mesh=mesh,
        in_specs=(
            P("section", "seq", None),
            P("section", "seq", None),
            P("section", None, None, None, None, None),
            P("section", None, None, None),
            P(),
            P("seq"),
            P("seq"),
        ),
        out_specs=(
            P("section", "seq", None),
            P("section", "seq", None),
            P("section", "seq", None, None),
            P("section", None, None, "seq", None, None),
        ),
        check_vma=False,
    )
```

time: 509 us -> 93.6 us (0.18)
  the two profiles are of different devices: /device:TPU:14 before, /device:TPU:6 now
where the time goes in v1:
time: 93.6 us; the launch traced here: 93.4 us
  Pallas kernels  86.2 us (92%)
  local copies, waits for them, and re-layouts  6.55 us (7%)
    pallas_call x1, Pallas kernels, body(): pl.pallas_call(functools.partial(kernel, nz, nsec), out_shape=(jax.ShapeD...  86.2 us
    unnamed x4, local copies, waits for them, and re-layouts  6.55 us

profile of v1, /device:TPU:6, one launch (start us, length us, event | category | flops | bytes accessed | tf_op | source)
XLA Modules:
  0.0 93.4 jit_solution(5060006460337242250)
XLA Ops:
  0.6 86.2 %shard_map.102 = (bf16[1,128,1024]{2,1,0:T(8,128)(2,1)}, bf16[1,128,1024]{2,1,0:T(8,128)(2,1)}, f32[1,32,2,1024]{3,2,1,0:T(2,128)}, f32[1,2,3,2,16,32]{5,4,3,2,1,0:T(8,128)}) custom-call(bf16[1,128,1024]{2,1,0:T(8,128)(2,1)} %refs_0_.1, bf16[1,128,1024]{2,1,0:T(8,128)(2,1)} %refs_1_.1, bf16[6,512,64]{2,1,0:T(8,128)(2,1)} %bitcast.8, ...), custom_call_target="tpu_custom_call" | custom-call | tf_op jit(solution)/shard_map/pallas_call | solution.py:438
  86.9 1.7 %copy.15 = bf16[1,128,1024]{2,1,0:T(8,128)(2,1)} copy(bf16[1,128,1024]{2,1,0:T(8,128)(2,1)} %get-tuple-element.8) | data formatting | bytes 524288
  88.5 1.7 %copy.16 = bf16[1,128,1024]{2,1,0:T(8,128)(2,1)} copy(bf16[1,128,1024]{2,1,0:T(8,128)(2,1)} %get-tuple-element.9) | data formatting | bytes 524288
  90.2 1.7 %copy.17 = f32[1,32,2,1024]{3,2,1,0:T(2,128)} copy(f32[1,32,2,1024]{3,2,1,0:T(2,128)} %get-tuple-element.10) | data formatting | bytes 524288
  91.9 1.5 %copy.18 = f32[1,2,3,2,16,32]{5,4,3,2,1,0:T(8,128)} copy(f32[1,2,3,2,16,32]{5,4,3,2,1,0:T(8,128)} %get-tuple-element.11) | data formatting | bytes 49152

commit v2 on v1

v2 whole, which is shorter than its diff:
```python
import functools

import jax
import jax.numpy as jnp
from jax import lax
from jax.experimental import pallas as pl
from jax.experimental.pallas import tpu as pltpu
from jax.sharding import PartitionSpec as P

MESH = pl.DeviceIdType.MESH
F32 = jnp.float32
BF = jnp.bfloat16
NY = 4
LANE = 128

NT = (((1,), (1,)), ((), ()))
TN = (((0,), (0,)), ((), ()))
NN = (((1,), (0,)), ((), ()))


def mm(a, b, dims):
    return lax.dot_general(a, b, dims, preferred_element_type=F32)


def iota(shape, dim):
    return lax.broadcasted_iota(jnp.int32, shape, dim)


def out_channel(col):
    return jnp.where(col < LANE, col & 15, 16 + (col & 15))


def expand_weights(kw, layer, wbd, groups):
    half = groups * 16 // 2
    sel = jnp.where(
        out_channel(iota((512, 256), 1)) == (iota((512, 256), 0) & 31), 1.0, 0.0
    ).astype(BF)
    keep_in = (iota((half, 512), 1) >> 5) == (iota((half, 512), 0) & 15)
    keep_group = ((iota((half, 256), 0) >> 4) & 7) == ((iota((half, 256), 1) & 127) >> 4)
    for part in range(2):
        pick = jnp.where(
            (iota((half, groups), 0) >> 4) + part * (groups // 2) == iota((half, groups), 1),
            1.0,
            0.0,
        ).astype(BF)
        for k in range(3):
            rows = mm(pick, kw[3 * layer + k], NT)
            rows = jnp.where(keep_in, rows, 0.0).astype(BF)
            full = jnp.where(keep_group, mm(rows, sel, NN), 0.0).astype(BF)
            for b in range(half // LANE):
                wbd[part * (half // LANE) + b, k * LANE : (k + 1) * LANE, :] = full[
                    b * LANE : (b + 1) * LANE
                ]


def kernel(nz, nsec, chunks, *refs):
    (x_in, cot_in, kw_in, mix_in, head_in, lab_in, ev_in) = refs[:7]
    (ig_out, nc_out, mg_out, cg_out) = refs[7:11]
    (ext, cot, kw, mix, head, lab, ev, wbd, gated, fac, mid, dpre, acc, snd_n, snd_f, rcv_n, rcv_f,
     tap1, tap2, hal_s, hal_r, nxt, gath, slc_s, slc_r, dlog, cnv_s, cnv_r, zown,
     lsem, ssem, rsem) = refs[11:43]
    zs0, zr0 = refs[43 : 43 + len(chunks)], refs[43 + len(chunks) : 43 + 2 * len(chunks)]
    ring_bufs = refs[43 + 2 * len(chunks) :]

    _, rows, chans = mid.shape
    nq = NY * nz
    rd = chans // nq
    blocks = chans // LANE
    per = LANE // rd
    groups = chans // 16
    sec = lax.axis_index("section")
    q = lax.axis_index("seq")
    y = lax.rem(q, NY)
    z = q // NY
    last = sec == nsec - 1

    def seq(step):
        return {"seq": lax.rem(q + step + nq, nq)}

    def ydev(step):
        return {"seq": z * NY + lax.rem(y + step, NY)}

    def zdev(step):
        return {"seq": lax.rem(z + step, nz) * NY + y}

    def lanes(b):
        return slice(b * LANE, (b + 1) * LANE)

    g, btw = gath.at[1, 0], gath.at[0, 0]
    own_x = ext.at[pl.ds(32, rows)]

    loads = []
    for i, (src, dst) in enumerate(
        [
            (x_in.at[0], own_x),
            (kw_in, kw),
            (mix_in.at[0, 0], mix.at[0]),
            (cot_in.at[0], cot),
            (mix_in.at[0, 1], mix.at[1]),
            (head_in, head),
            (lab_in, lab),
            (ev_in, ev),
        ]
    ):
        copy = pltpu.make_async_copy(src, dst, lsem.at[i])
        copy.start()
        loads.append(copy)

    sends = []

    def push(src, dst, target):
        n = len(sends)
        copy = pltpu.make_async_remote_copy(
            src_ref=src,
            dst_ref=dst,
            send_sem=ssem.at[n],
            recv_sem=rsem.at[n],
            device_id=target,
            device_id_type=MESH,
        )
        copy.start()
        sends.append(copy)
        return copy

    def got(copies):
        for c in copies:
            c.wait_recv()

    barrier = pltpu.get_barrier_semaphore()
    greet = [seq(-1), seq(-2), seq(1), seq(2)]
    greet += [ydev(j) for j in range(1, NY)] + [zdev(j) for j in range(1, nz)]
    greet.append({"section": lax.rem(sec + 1, nsec)})
    for target in greet:
        pl.semaphore_signal(barrier, inc=1, device_id=target, device_id_type=MESH)
    pl.semaphore_wait(barrier, len(greet))

    def share(src, dst):
        return [push(src(j), dst(j), ydev(j)) for j in range(1, NY)]

    loads[0].wait()
    halo = [push(ext.at[pl.ds(rows, 32)], ext.at[pl.ds(0, 32)], seq(1))]
    loads[3].wait()
    cots = share(lambda j: cot, lambda j: gath.at[1, j])
    g[...] = cot[...]

    loads[1].wait()
    expand_weights(kw, 0, wbd.at[0], groups)
    loads[2].wait()
    got(halo)

    @pl.when(q == 0)
    def _():
        ext[0:32] = jnp.zeros((32, chans), BF)

    def taps_short(b):
        return jnp.concatenate(
            [ext[32 : 32 + rows, lanes(b)], ext[16 : 16 + rows, lanes(b)], ext[0:rows, lanes(b)]],
            axis=1,
        )

    def taps_long(b):
        return jnp.concatenate([mid[i, :, lanes(b)] for i in range(3)], axis=1)

    def gates(layer, taps):
        for b in range(blocks):
            pre = mm(taps(b), wbd[layer, b], NN).astype(BF).astype(F32)
            filt = jnp.tanh(pre[:, :LANE])
            gate = jax.nn.sigmoid(pre[:, LANE:])
            gated[layer, :, lanes(b)] = (filt * gate).astype(BF)
            fac[layer, 0, :, lanes(b)] = gate * (1.0 - filt * filt)
            fac[layer, 1, :, lanes(b)] = filt * gate * (1.0 - gate)

    def turn(layer):
        for b in range(blocks):
            turned = gated[layer, :, lanes(b)].T
            for i in range(per):
                d = b * per + i
                slc_s[layer, d % NY, d // NY] = turned[i * rd : (i + 1) * rd]

    def share_slices(layer):
        slc_r[layer, 0] = slc_s[layer, y]
        return share(
            lambda j: slc_s.at[layer, lax.rem(y + j, NY)], lambda j: slc_r.at[layer, j]
        )

    gates(0, taps_short)
    mid[0] = (ext[32 : 32 + rows].astype(F32) + mm(gated[0], mix[0], NN)).astype(BF)
    forth = [push(mid.at[0], mid.at[2], seq(NY)), push(mid.at[0], mid.at[1], seq(2))]

    expand_weights(kw, 1, wbd.at[1], groups)
    turn(0)
    for copy in loads[4:]:
        copy.wait()
    got(forth)
    slices0 = share_slices(0)

    @pl.when(q < 2)
    def _():
        mid[1] = jnp.zeros((rows, chans), BF)

    @pl.when(q < NY)
    def _():
        mid[2] = jnp.zeros((rows, chans), BF)

    gates(1, taps_long)
    turn(1)
    slices1 = share_slices(1)

    def add_loss(ref, grad):
        ref[...] = (ref[...].astype(F32) + mm(grad, head[...], TN)).astype(BF)

    dlog[0] = jnp.zeros(dlog.shape[1:], BF)

    @pl.when(last)
    def _():
        top = (mid[0].astype(F32) + mm(gated[1], mix[1], NN)).astype(BF)
        hazard = jax.nn.sigmoid(mm(head[...], top, NT))
        bins = iota(hazard.shape, 0)
        below = jnp.where(bins <= lab[...], hazard, 0.0)
        at_label = jnp.where(bins == lab[...], ev[...].astype(F32), 0.0)
        dlog[0] = (below - at_label).astype(BF)
        add_loss(g, dlog[0])

    losses = share(lambda j: dlog.at[0], lambda j: dlog.at[j])

    def cot_of_pre(layer, upstream):
        dgated = mm(upstream, mix[layer], NT)
        for b in range(blocks):
            both = jnp.concatenate(
                [
                    dgated[:, lanes(b)] * fac[layer, 0, :, lanes(b)],
                    dgated[:, lanes(b)] * fac[layer, 1, :, lanes(b)],
                ],
                axis=1,
            ).astype(BF)
            dpre[layer, :, 256 * b : 256 * (b + 1)] = both

    def back_taps(layer, b):
        return mm(dpre[layer, :, 256 * b : 256 * (b + 1)], wbd[layer, b], NT)

    cot_of_pre(1, g[...])
    for b in range(blocks):
        prods = back_taps(1, b)
        acc[:, lanes(b)] = prods[:, :LANE]
        snd_n[:, lanes(b)] = prods[:, LANE : 2 * LANE].astype(BF)
        snd_f[:, lanes(b)] = prods[:, 2 * LANE :].astype(BF)
    back = [push(snd_f, rcv_f, seq(-NY)), push(snd_n, rcv_n, seq(-2))]

    compact = jnp.where(
        iota((768, LANE), 1) == 32 * (iota((768, LANE), 0) >> 8) + out_channel(iota((768, LANE), 0) & 255),
        1.0,
        0.0,
    ).astype(BF)
    own_group = (iota((LANE, 256), 0) >> 4) == ((iota((LANE, 256), 1) & 127) >> 4)

    def conv_terms(layer, taps):
        for b in range(blocks):
            full = mm(taps(b), dpre[layer, :, 256 * b : 256 * (b + 1)], TN)
            kept = jnp.concatenate(
                [
                    jnp.where(own_group, full[k * LANE : (k + 1) * LANE], 0.0).astype(BF)
                    for k in range(3)
                ],
                axis=1,
            )
            packed = mm(kept, compact, NN).astype(BF)
            for i in range(per):
                d = b * per + i
                cnv_s[layer, d % NY, d // NY] = packed[i * rd : (i + 1) * rd]
        return share(
            lambda j: cnv_s.at[layer, lax.rem(y + j, NY)], lambda j: cnv_r.at[layer, j - 1]
        )

    convs1 = conv_terms(1, taps_long)

    def quarter(layer, lo, w):
        left = jnp.concatenate(
            [slc_r[layer, j].reshape(nz * rd, rows) for j in range(NY)], axis=1
        )
        right = gath[layer, :, :, lo : lo + w].reshape(NY * rows, w)
        return mm(left, right, NN).reshape(nz, rd, w)

    def spread(buf, dst):
        return [
            push(buf.at[lax.rem(z + j, nz)], dst.at[j - 1], zdev(j)) for j in range(1, nz)
        ]

    got(slices1)
    got(cots)
    got(losses)

    @pl.when(last)
    def _():
        for j in range(1, NY):
            add_loss(gath.at[1, j], dlog[j])

    def ring(own, done):
        right_s, right_r, left_s, left_r = ring_bufs
        arrived, at = None, 0
        for t in range(1, nz // 2 + 1):
            dist = nz // 2 - t + 1
            to_r, to_l = lax.rem(z + dist, nz), lax.rem(z - dist + nz, nz)
            size = 1 if t == 1 else 2
            if arrived is not None:
                was, copies = arrived
                got(copies)
            for d in range(2):
                if t > 1 or d == 0:
                    v = own(to_r, d)
                    if t > 2 or (t == 2 and d == 0):
                        v = v + right_r[was + d].astype(F32)
                    right_s[at + d] = v.astype(BF)
                if t > 1 or d == 1:
                    v = own(to_l, d)
                    if t > 2 or (t == 2 and d == 1):
                        v = v + left_r[was + (0 if t == 2 else d)].astype(F32)
                    left_s[at + (0 if t == 1 else d)] = v.astype(BF)
            copies = [
                push(right_s.at[pl.ds(at, size)], right_r.at[pl.ds(at, size)], zdev(1)),
                push(left_s.at[pl.ds(at, size)], left_r.at[pl.ds(at, size)], zdev(nz - 1)),
            ]
            arrived = (at, copies)
            at += size
            yield
        was, copies = arrived
        got(copies)
        for d in range(2):
            v = own(z, d)
            if nz > 2:
                v = v + right_r[was + d].astype(F32) + left_r[was + d].astype(F32)
            elif d == 0:
                v = v + right_r[was].astype(F32)
            else:
                v = v + left_r[was].astype(F32)
            done(d, v)
        yield

    half = rd // 2
    for lo in range(0, chans, 256):
        zown[1, :, :, lo : lo + 256] = quarter(1, lo, 256)

    def conv_sum(layer, copies):
        got(copies)
        sums = cnv_s[layer, y].astype(F32)
        for j in range(NY - 1):
            sums = sums + cnv_r[layer, j].astype(F32)
        zown[layer, :, :, chans : chans + LANE] = sums
        return sums

    def put_conv(layer, lo, sums):
        for k in range(3):
            cg_out[0, layer, k, lo // 16 : (lo + sums.shape[0]) // 16] = sums[
                :, 32 * k : 32 * (k + 1)
            ].reshape(sums.shape[0] // 16, 16, 32)

    def finish1(d, v):
        mg_out[0, d * half : (d + 1) * half, 1, :] = v[:, 0:chans]
        put_conv(1, d * half, v[:, chans:])

    conv_sum(1, convs1)
    ring1 = ring(lambda e, d: zown[1, e, d * half : (d + 1) * half, :], finish1)
    next(ring1, None)

    got(back)

    @pl.when(q >= nq - 2)
    def _():
        rcv_n[...] = jnp.zeros((rows, chans), BF)

    @pl.when(q >= nq - NY)
    def _():
        rcv_f[...] = jnp.zeros((rows, chans), BF)

    btw[...] = (
        g[...].astype(F32) + acc[...] + rcv_n[...].astype(F32) + rcv_f[...].astype(F32)
    ).astype(BF)
    shared = [
        share(
            lambda j: gath.at[0, 0, :, pl.ds(lo, w)], lambda j: gath.at[0, j, :, pl.ds(lo, w)]
        )
        for lo, w, _ in chunks
    ]

    next(ring1, None)
    cot_of_pre(0, btw[...])
    for b in range(blocks):
        prods = back_taps(0, b)
        acc[:, lanes(b)] = prods[:, :LANE]
        tap1[0:rows, lanes(b)] = prods[:, LANE : 2 * LANE]
        tap2[0:rows, lanes(b)] = prods[:, 2 * LANE :]
    hal_s[0:16] = tap2[0:16].astype(BF)
    hal_s[16:32] = (tap1[0:16] + tap2[16:32]).astype(BF)
    back_halo = push(hal_s, hal_r, seq(-1))
    convs0 = conv_terms(0, taps_short)
    next(ring1, None)
    tap1[rows : rows + 16] = jnp.zeros((16, chans), F32)
    tap2[rows : rows + 32] = jnp.zeros((32, chans), F32)
    back_halo.wait_recv()

    @pl.when(q == nq - 1)
    def _():
        hal_r[...] = jnp.zeros((32, chans), BF)

    total = btw[...].astype(F32) + acc[...] + tap1[16 : 16 + rows] + tap2[32 : 32 + rows]
    ig_out[0, 0 : rows - 32] = total[0 : rows - 32].astype(BF)
    ig_out[0, rows - 32 : rows] = (total[rows - 32 :] + hal_r[...].astype(F32)).astype(BF)
    to_prev = push(ig_out.at[0], nxt, {"section": lax.rem(sec + nsec - 1, nsec)})

    got(slices0)
    over0 = []
    for c, (lo, w, conv) in enumerate(chunks):
        got(shared[c])
        block = quarter(0, lo, w)
        zown[0, :, :, lo : lo + w] = block
        zs0[c][:, :, 0:w] = block.astype(BF)
        if conv:
            zs0[c][:, :, w : w + LANE] = conv_sum(0, convs0).astype(BF)
        over0.append(spread(zs0[c], zr0[c]))
        if c == 0:
            next(ring1, None)
    for _ in range(nz // 2 - 3):
        next(ring1, None)

    def total_of(own, bufs, lo, w):
        v = own
        for j in range(nz - 1):
            v = v + bufs[j, :, lo : lo + w].astype(F32)
        return v

    to_prev.wait_recv()

    @pl.when(last)
    def _():
        nc_out[0] = g[...]

    @pl.when(jnp.logical_not(last))
    def _():
        nc_out[0] = nxt[...]

    for c, (lo, w, conv) in enumerate(chunks):
        got(over0[c])
        mg_out[0, :, 0, lo : lo + w] = total_of(zown[0, z, :, lo : lo + w], zr0[c], 0, w)
        if conv:
            put_conv(0, 0, total_of(zown[0, z, :, chans : chans + LANE], zr0[c], w, LANE))

    for copy in sends:
        copy.wait_send()


def hand_over(*refs):
    srcs, dsts, bufs, (sem_in, sem_out) = refs[:4], refs[4:8], refs[8:12], refs[12:]
    fetch = [pltpu.make_async_copy(a, b, sem_in.at[i]) for i, (a, b) in enumerate(zip(srcs, bufs))]
    store = [pltpu.make_async_copy(a, b, sem_out.at[i]) for i, (a, b) in enumerate(zip(bufs, dsts))]
    for copy in fetch:
        copy.start()
    for before, after in zip(fetch, store):
        before.wait()
        after.start()
    for copy in store:
        copy.wait()


def solution(mesh):
    nsec, nq = mesh.shape["section"], mesh.shape["seq"]
    nz = nq // NY

    def body(x, cot, kernel_weight, blend, head, labels, events):
        _, rows, chans = x.shape
        groups, gin, gout = kernel_weight.shape[3:]
        rd = chans // nq
        blocks = chans // LANE
        kw = jnp.transpose(kernel_weight[0], (0, 1, 3, 4, 2)).reshape(6, gin * gout, groups)
        any_ = pl.BlockSpec(memory_space=pl.ANY)
        vm = pl.BlockSpec(memory_space=pltpu.VMEM)
        act = pltpu.VMEM((rows, chans), BF)
        step = chans // 4
        chunks = [(i * step, step, i == 3) for i in range(4)]
        wide = [w + (LANE if conv else 0) for _, w, conv in chunks]
        n_push = 1 + 3 + 2 + 6 + 3 + 2 + 6 + nz + 12 + 2 + 4 * (nz - 1)
        bins = head.shape[1]
        scratch = [
            pltpu.VMEM((rows + 32, chans), BF),
            act,
            pltpu.VMEM((6, gin * gout, groups), BF),
            pltpu.VMEM((2, chans, chans), BF),
            pltpu.VMEM((bins, chans), BF),
            pltpu.VMEM((1, rows), jnp.int32),
            pltpu.VMEM((1, rows), jnp.int32),
            pltpu.VMEM((2, blocks, 3 * LANE, 2 * LANE), BF),
            pltpu.VMEM((2, rows, chans), BF),
            pltpu.VMEM((2, 2, rows, chans), F32),
            pltpu.VMEM((3, rows, chans), BF),
            pltpu.VMEM((2, rows, 2 * chans), BF),
            pltpu.VMEM((rows, chans), F32),
            act,
            act,
            act,
            act,
            pltpu.VMEM((rows + 16, chans), F32),
            pltpu.VMEM((rows + 32, chans), F32),
            pltpu.VMEM((32, chans), BF),
            pltpu.VMEM((32, chans), BF),
            act,
            pltpu.VMEM((2, NY, rows, chans), BF),
            pltpu.VMEM((2, NY, nz, rd, rows), BF),
            pltpu.VMEM((2, NY, nz, rd, rows), BF),
            pltpu.VMEM((NY, bins, rows), BF),
            pltpu.VMEM((2, NY, nz, rd, LANE), BF),
            pltpu.VMEM((2, NY - 1, nz, rd, LANE), BF),
            pltpu.VMEM((2, nz, rd, chans + LANE), F32),
            pltpu.SemaphoreType.DMA((8,)),
            pltpu.SemaphoreType.DMA((n_push,)),
            pltpu.SemaphoreType.DMA((n_push,)),
        ]
        scratch += [pltpu.VMEM((nz, rd, w), BF) for w in wide]
        scratch += [pltpu.VMEM((nz - 1, rd, w), BF) for w in wide]
        scratch += [pltpu.VMEM((nz - 1, rd // 2, chans + LANE), BF)] * 4
        shapes = (
            jax.ShapeDtypeStruct((1, rows, chans), BF),
            jax.ShapeDtypeStruct((1, rows, chans), BF),
            jax.ShapeDtypeStruct((1, rd, 2, chans), F32),
            jax.ShapeDtypeStruct((1, 2, 3, groups // nq, gin, gout), F32),
        )
        outs = pl.pallas_call(
            functools.partial(kernel, nz, nsec, chunks),
            out_shape=shapes,
            in_specs=[any_] * 7,
            out_specs=(vm, vm, vm, vm),
            scratch_shapes=scratch,
            compiler_params=pltpu.CompilerParams(
                collective_id=0, has_side_effects=True, vmem_limit_bytes=58 * 1024 * 1024
            ),
        )(x, cot, kw, blend, head.T, labels.reshape(1, rows), events.reshape(1, rows))
        return pl.pallas_call(
            hand_over,
            out_shape=shapes,
            in_specs=[any_] * 4,
            out_specs=(any_,) * 4,
            scratch_shapes=[pltpu.VMEM(o.shape, o.dtype) for o in shapes]
            + [pltpu.SemaphoreType.DMA((4,))] * 2,
        )(*outs)

    return jax.shard_map(
        body,
        mesh=mesh,
        in_specs=(
            P("section", "seq", None),
            P("section", "seq", None),
            P("section", None, None, None, None, None),
            P("section", None, None, None),
            P(),
            P("seq"),
            P("seq"),
        ),
        out_specs=(
            P("section", "seq", None),
            P("section", "seq", None),
            P("section", "seq", None, None),
            P("section", None, None, "seq", None, None),
        ),
        check_vma=False,
    )
```

time: 93.6 us -> 78.4 us (0.84)
  the two profiles are of different devices: /device:TPU:6 before, /device:TPU:14 now
where the time goes in v2:
time: 78.4 us; the launch traced here: 78.3 us
  Pallas kernels  77.6 us (99%)
    pallas_call x1, Pallas kernels, body(): pl.pallas_call(functools.partial(kernel, nz, nsec, chunks), out_shape=sha...  75.7 us
    pallas_call x1, Pallas kernels, body(): pl.pallas_call(hand_over, out_shape=shapes, in_specs=[any_] * 4, out_spec...  1.92 us

profile of v2, /device:TPU:14, one launch (start us, length us, event | category | flops | bytes accessed | tf_op | source)
XLA Modules:
  0.0 78.3 jit_solution(8741443791658372290)
XLA Ops:
  0.6 75.7 %shard_map.102 = (bf16[1,128,1024]{2,1,0:T(8,128)(2,1)}, bf16[1,128,1024]{2,1,0:T(8,128)(2,1)}, f32[1,32,2,1024]{3,2,1,0:T(2,128)}, f32[1,2,3,2,16,32]{5,4,3,2,1,0:T(8,128)}) custom-call(bf16[1,128,1024]{2,1,0:T(8,128)(2,1)} %refs_0_.1, bf16[1,128,1024]{2,1,0:T(8,128)(2,1)} %refs_1_.1, bf16[6,512,64]{2,1,0:T(8,128)(2,1)} %bitcast.8, ...), custom_call_target="tpu_custom_call" | custom-call | tf_op jit(solution)/shard_map/pallas_call | solution.py:524
  76.4 1.9 %shard_map.103 = (bf16[1,128,1024]{2,1,0:T(8,128)(2,1)}, bf16[1,128,1024]{2,1,0:T(8,128)(2,1)}, f32[1,32,2,1024]{3,2,1,0:T(2,128)}, f32[1,2,3,2,16,32]{5,4,3,2,1,0:T(8,128)}) custom-call(bf16[1,128,1024]{2,1,0:T(8,128)(2,1)} %get-tuple-element.8.refs_0_, bf16[1,128,1024]{2,1,0:T(8,128)(2,1)} %get-tuple-element.9.refs_1_, ...), custom_call_target="tpu_custom_call" | custom-call | tf_op jit(solution)/shard_map/pallas_call | solution.py:534

commit v3 on v2

--- a/solution.py
+++ b/solution.py
@@ -137,10 +137,21 @@
     def share(src, dst):
         return [push(src(j), dst(j), ydev(j)) for j in range(1, NY)]
 
+    def gather_near(own, slot):
+        return [push(own, slot(1), ydev(1)), push(own, slot(NY - 1), ydev(NY - 1))]
+
+    def gather_far(copies, slot):
+        on = []
+        for copy, j, at in ((copies[0], 1, 0), (copies[1], NY - 1, rows // 2)):
+            got([copy])
+            part = pl.ds(at, rows // 2)
+            on.append(push(slot(j).at[part], slot(2).at[part], ydev(j)))
+        return on
+
     loads[0].wait()
     halo = [push(ext.at[pl.ds(rows, 32)], ext.at[pl.ds(0, 32)], seq(1))]
     loads[3].wait()
-    cots = share(lambda j: cot, lambda j: gath.at[1, j])
+    cots = gather_near(cot, lambda j: gath.at[1, j])
     g[...] = cot[...]
 
     loads[1].wait()
@@ -187,12 +198,13 @@
     mid[0] = (ext[32 : 32 + rows].astype(F32) + mm(gated[0], mix[0], NN)).astype(BF)
     forth = [push(mid.at[0], mid.at[2], seq(NY)), push(mid.at[0], mid.at[1], seq(2))]
 
+    cots = gather_far(cots, lambda j: gath.at[1, j])
+    turn(0)
+    slices0 = share_slices(0)
     expand_weights(kw, 1, wbd.at[1], groups)
-    turn(0)
     for copy in loads[4:]:
         copy.wait()
     got(forth)
-    slices0 = share_slices(0)
 
     @pl.when(q < 2)
     def _():
@@ -203,8 +215,6 @@
         mid[2] = jnp.zeros((rows, chans), BF)
 
     gates(1, taps_long)
-    turn(1)
-    slices1 = share_slices(1)
 
     def add_loss(ref, grad):
         ref[...] = (ref[...].astype(F32) + mm(grad, head[...], TN)).astype(BF)
@@ -245,6 +255,8 @@
         snd_n[:, lanes(b)] = prods[:, LANE : 2 * LANE].astype(BF)
         snd_f[:, lanes(b)] = prods[:, 2 * LANE :].astype(BF)
     back = [push(snd_f, rcv_f, seq(-NY)), push(snd_n, rcv_n, seq(-2))]
+    turn(1)
+    slices1 = share_slices(1)
 
     compact = jnp.where(
         iota((768, LANE), 1) == 32 * (iota((768, LANE), 0) >> 8) + out_channel(iota((768, LANE), 0) & 255),
@@ -288,6 +300,8 @@
     got(slices1)
     got(cots)
     got(losses)
+    for copy in cots:
+        copy.wait_send()
 
     @pl.when(last)
     def _():
@@ -374,13 +388,11 @@
     btw[...] = (
         g[...].astype(F32) + acc[...] + rcv_n[...].astype(F32) + rcv_f[...].astype(F32)
     ).astype(BF)
-    shared = [
-        share(
-            lambda j: gath.at[0, 0, :, pl.ds(lo, w)], lambda j: gath.at[0, j, :, pl.ds(lo, w)]
-        )
-        for lo, w, _ in chunks
-    ]
-
+    def lane_slot(lo, w):
+        return lambda j: gath.at[0, j, :, pl.ds(lo, w)]
+
+    slots = [lane_slot(lo, w) for lo, w, _ in chunks]
+    shared = [gather_near(slot(0), slot) for slot in slots]
     next(ring1, None)
     cot_of_pre(0, btw[...])
     for b in range(blocks):
@@ -391,7 +403,9 @@
     hal_s[0:16] = tap2[0:16].astype(BF)
     hal_s[16:32] = (tap1[0:16] + tap2[16:32]).astype(BF)
     back_halo = push(hal_s, hal_r, seq(-1))
+    shared[0] = gather_far(shared[0], slots[0])
     convs0 = conv_terms(0, taps_short)
+    shared[1] = gather_far(shared[1], slots[1])
     next(ring1, None)
     tap1[rows : rows + 16] = jnp.zeros((16, chans), F32)
     tap2[rows : rows + 32] = jnp.zeros((32, chans), F32)
@@ -406,6 +420,8 @@
     ig_out[0, rows - 32 : rows] = (total[rows - 32 :] + hal_r[...].astype(F32)).astype(BF)
     to_prev = push(ig_out.at[0], nxt, {"section": lax.rem(sec + nsec - 1, nsec)})
 
+    for c in range(2, len(chunks)):
+        shared[c] = gather_far(shared[c], slots[c])
     got(slices0)
     over0 = []
     for c, (lo, w, conv) in enumerate(chunks):
@@ -444,7 +460,8 @@
             put_conv(0, 0, total_of(zown[0, z, :, chans : chans + LANE], zr0[c], w, LANE))
 
     for copy in sends:
-        copy.wait_send()
+        if all(copy is not c for c in cots):
+            copy.wait_send()
 
 
 def hand_over(*refs):
@@ -473,10 +490,10 @@
         any_ = pl.BlockSpec(memory_space=pl.ANY)
         vm = pl.BlockSpec(memory_space=pltpu.VMEM)
         act = pltpu.VMEM((rows, chans), BF)
-        step = chans // 4
-        chunks = [(i * step, step, i == 3) for i in range(4)]
+        quarter = chans // 4
+        chunks = [(0, 2 * quarter, False), (2 * quarter, quarter, False), (3 * quarter, quarter, True)]
         wide = [w + (LANE if conv else 0) for _, w, conv in chunks]
-        n_push = 1 + 3 + 2 + 6 + 3 + 2 + 6 + nz + 12 + 2 + 4 * (nz - 1)
+        n_push = 1 + 4 + 2 + 6 + 3 + 2 + 6 + nz + 16 + 2 + 4 * (nz - 1)
         bins = head.shape[1]
         scratch = [
             pltpu.VMEM((rows + 32, chans), BF),

time: 78.4 us -> 71.2 us (0.908)
  Pallas kernels: 77.6 us -> 70.5 us
    pallas_call x1, Pallas kernels: 75.7 us -> 68.5 us  [body(): pl.pallas_call(functools.partial(kernel, nz, nsec, chunks), out_shape=sha...]
where the time goes in v3:
time: 71.2 us; the launch traced here: 71.1 us
  Pallas kernels  70.5 us (99%)
    pallas_call x1, Pallas kernels, body(): pl.pallas_call(functools.partial(kernel, nz, nsec, chunks), out_shape=sha...  68.5 us
    pallas_call x1, Pallas kernels, body(): pl.pallas_call(hand_over, out_shape=shapes, in_specs=[any_] * 4, out_spec...  1.92 us

profile of v3, /device:TPU:14, one launch (start us, length us, event | category | flops | bytes accessed | tf_op | source)
XLA Modules:
  0.0 71.1 jit_solution(14318771152477051130)
XLA Ops:
  0.6 68.5 %shard_map.102 = (bf16[1,128,1024]{2,1,0:T(8,128)(2,1)}, bf16[1,128,1024]{2,1,0:T(8,128)(2,1)}, f32[1,32,2,1024]{3,2,1,0:T(2,128)}, f32[1,2,3,2,16,32]{5,4,3,2,1,0:T(8,128)}) custom-call(bf16[1,128,1024]{2,1,0:T(8,128)(2,1)} %refs_0_.1, bf16[1,128,1024]{2,1,0:T(8,128)(2,1)} %refs_1_.1, bf16[6,512,64]{2,1,0:T(8,128)(2,1)} %bitcast.8, ...), custom_call_target="tpu_custom_call" | custom-call | tf_op jit(solution)/shard_map/pallas_call | solution.py:541
  69.2 1.9 %shard_map.103 = (bf16[1,128,1024]{2,1,0:T(8,128)(2,1)}, bf16[1,128,1024]{2,1,0:T(8,128)(2,1)}, f32[1,32,2,1024]{3,2,1,0:T(2,128)}, f32[1,2,3,2,16,32]{5,4,3,2,1,0:T(8,128)}) custom-call(bf16[1,128,1024]{2,1,0:T(8,128)(2,1)} %get-tuple-element.8.refs_0_, bf16[1,128,1024]{2,1,0:T(8,128)(2,1)} %get-tuple-element.9.refs_1_, ...), custom_call_target="tpu_custom_call" | custom-call | tf_op jit(solution)/shard_map/pallas_call | solution.py:551

commit v4 on v3

--- a/solution.py
+++ b/solution.py
@@ -58,9 +58,9 @@
     (ig_out, nc_out, mg_out, cg_out) = refs[7:11]
     (ext, cot, kw, mix, head, lab, ev, wbd, gated, fac, mid, dpre, acc, snd_n, snd_f, rcv_n, rcv_f,
      tap1, tap2, hal_s, hal_r, nxt, gath, slc_s, slc_r, dlog, cnv_s, cnv_r, zown,
-     lsem, ssem, rsem) = refs[11:43]
-    zs0, zr0 = refs[43 : 43 + len(chunks)], refs[43 + len(chunks) : 43 + 2 * len(chunks)]
-    ring_bufs = refs[43 + 2 * len(chunks) :]
+     lsem, ssem, rsem, ig_buf, nc_buf, mg_buf, cg_buf, osem) = refs[11:48]
+    zs0, zr0 = refs[48 : 48 + len(chunks)], refs[48 + len(chunks) : 48 + 2 * len(chunks)]
+    ring_bufs = refs[48 + 2 * len(chunks) :]
 
     _, rows, chans = mid.shape
     nq = NY * nz
@@ -363,12 +363,12 @@
 
     def put_conv(layer, lo, sums):
         for k in range(3):
-            cg_out[0, layer, k, lo // 16 : (lo + sums.shape[0]) // 16] = sums[
+            cg_buf[0, layer, k, lo // 16 : (lo + sums.shape[0]) // 16] = sums[
                 :, 32 * k : 32 * (k + 1)
             ].reshape(sums.shape[0] // 16, 16, 32)
 
     def finish1(d, v):
-        mg_out[0, d * half : (d + 1) * half, 1, :] = v[:, 0:chans]
+        mg_buf[0, d * half : (d + 1) * half, 1, :] = v[:, 0:chans]
         put_conv(1, d * half, v[:, chans:])
 
     conv_sum(1, convs1)
@@ -416,9 +416,15 @@
         hal_r[...] = jnp.zeros((32, chans), BF)
 
     total = btw[...].astype(F32) + acc[...] + tap1[16 : 16 + rows] + tap2[32 : 32 + rows]
-    ig_out[0, 0 : rows - 32] = total[0 : rows - 32].astype(BF)
-    ig_out[0, rows - 32 : rows] = (total[rows - 32 :] + hal_r[...].astype(F32)).astype(BF)
-    to_prev = push(ig_out.at[0], nxt, {"section": lax.rem(sec + nsec - 1, nsec)})
+    ig_buf[0, 0 : rows - 32] = total[0 : rows - 32].astype(BF)
+    ig_buf[0, rows - 32 : rows] = (total[rows - 32 :] + hal_r[...].astype(F32)).astype(BF)
+    def write(i, src, dst):
+        copy = pltpu.make_async_copy(src, dst, osem.at[i])
+        copy.start()
+        return copy
+
+    writes = [write(0, ig_buf, ig_out)]
+    to_prev = push(ig_buf.at[0], nxt, {"section": lax.rem(sec + nsec - 1, nsec)})
 
     for c in range(2, len(chunks)):
         shared[c] = gather_far(shared[c], slots[c])
@@ -447,18 +453,23 @@
 
     @pl.when(last)
     def _():
-        nc_out[0] = g[...]
+        nc_buf[0] = g[...]
 
     @pl.when(jnp.logical_not(last))
     def _():
-        nc_out[0] = nxt[...]
+        nc_buf[0] = nxt[...]
+
+    writes.append(write(1, nc_buf, nc_out))
 
     for c, (lo, w, conv) in enumerate(chunks):
         got(over0[c])
-        mg_out[0, :, 0, lo : lo + w] = total_of(zown[0, z, :, lo : lo + w], zr0[c], 0, w)
+        mg_buf[0, :, 0, lo : lo + w] = total_of(zown[0, z, :, lo : lo + w], zr0[c], 0, w)
         if conv:
             put_conv(0, 0, total_of(zown[0, z, :, chans : chans + LANE], zr0[c], w, LANE))
 
+    writes += [write(2, mg_buf, mg_out), write(3, cg_buf, cg_out)]
+    for copy in writes:
+        copy.wait()
     for copy in sends:
         if all(copy is not c for c in cots):
             copy.wait_send()
@@ -529,20 +540,21 @@
             pltpu.SemaphoreType.DMA((n_push,)),
             pltpu.SemaphoreType.DMA((n_push,)),
         ]
-        scratch += [pltpu.VMEM((nz, rd, w), BF) for w in wide]
-        scratch += [pltpu.VMEM((nz - 1, rd, w), BF) for w in wide]
-        scratch += [pltpu.VMEM((nz - 1, rd // 2, chans + LANE), BF)] * 4
         shapes = (
             jax.ShapeDtypeStruct((1, rows, chans), BF),
             jax.ShapeDtypeStruct((1, rows, chans), BF),
             jax.ShapeDtypeStruct((1, rd, 2, chans), F32),
             jax.ShapeDtypeStruct((1, 2, 3, groups // nq, gin, gout), F32),
         )
+        scratch += [pltpu.VMEM(o.shape, o.dtype) for o in shapes] + [pltpu.SemaphoreType.DMA((4,))]
+        scratch += [pltpu.VMEM((nz, rd, w), BF) for w in wide]
+        scratch += [pltpu.VMEM((nz - 1, rd, w), BF) for w in wide]
+        scratch += [pltpu.VMEM((nz - 1, rd // 2, chans + LANE), BF)] * 4
         outs = pl.pallas_call(
             functools.partial(kernel, nz, nsec, chunks),
             out_shape=shapes,
             in_specs=[any_] * 7,
-            out_specs=(vm, vm, vm, vm),
+            out_specs=(any_,) * 4,
             scratch_shapes=scratch,
             compiler_params=pltpu.CompilerParams(
                 collective_id=0, has_side_effects=True, vmem_limit_bytes=58 * 1024 * 1024

time: 71.2 us -> 71 us (level)
  no operation moved by 1% of the time
where the time goes in v4:
time: 71 us; the launch traced here: 70.9 us
  Pallas kernels  70.2 us (99%)
    pallas_call x1, Pallas kernels, body(): pl.pallas_call(functools.partial(kernel, nz, nsec, chunks), out_shape=sha...  68.3 us
    pallas_call x1, Pallas kernels, body(): pl.pallas_call(hand_over, out_shape=shapes, in_specs=[any_] * 4, out_spec...  1.92 us

profile of v4, /device:TPU:14, one launch (start us, length us, event | category | flops | bytes accessed | tf_op | source)
XLA Modules:
  0.0 70.9 jit_solution(6101382870420000151)
XLA Ops:
  0.6 68.3 %shard_map.102 = (bf16[1,128,1024]{2,1,0:T(8,128)(2,1)}, bf16[1,128,1024]{2,1,0:T(8,128)(2,1)}, f32[1,32,2,1024]{3,2,1,0:T(2,128)}, f32[1,2,3,2,16,32]{5,4,3,2,1,0:T(8,128)}) custom-call(bf16[1,128,1024]{2,1,0:T(8,128)(2,1)} %refs_0_.1, bf16[1,128,1024]{2,1,0:T(8,128)(2,1)} %refs_1_.1, bf16[6,512,64]{2,1,0:T(8,128)(2,1)} %bitcast.8, ...), custom_call_target="tpu_custom_call" | custom-call | tf_op jit(solution)/shard_map/pallas_call | solution.py:553
  68.9 1.9 %shard_map.103 = (bf16[1,128,1024]{2,1,0:T(8,128)(2,1)}, bf16[1,128,1024]{2,1,0:T(8,128)(2,1)}, f32[1,32,2,1024]{3,2,1,0:T(2,128)}, f32[1,2,3,2,16,32]{5,4,3,2,1,0:T(8,128)}) custom-call(bf16[1,128,1024]{2,1,0:T(8,128)(2,1)} %get-tuple-element.8.refs_0_, bf16[1,128,1024]{2,1,0:T(8,128)(2,1)} %get-tuple-element.9.refs_1_, ...), custom_call_target="tpu_custom_call" | custom-call | tf_op jit(solution)/shard_map/pallas_call | solution.py:563

commit v5 on v4

--- a/solution.py
+++ b/solution.py
@@ -409,28 +409,13 @@
     next(ring1, None)
     tap1[rows : rows + 16] = jnp.zeros((16, chans), F32)
     tap2[rows : rows + 32] = jnp.zeros((32, chans), F32)
-    back_halo.wait_recv()
-
-    @pl.when(q == nq - 1)
-    def _():
-        hal_r[...] = jnp.zeros((32, chans), BF)
-
-    total = btw[...].astype(F32) + acc[...] + tap1[16 : 16 + rows] + tap2[32 : 32 + rows]
-    ig_buf[0, 0 : rows - 32] = total[0 : rows - 32].astype(BF)
-    ig_buf[0, rows - 32 : rows] = (total[rows - 32 :] + hal_r[...].astype(F32)).astype(BF)
-    def write(i, src, dst):
-        copy = pltpu.make_async_copy(src, dst, osem.at[i])
-        copy.start()
-        return copy
-
-    writes = [write(0, ig_buf, ig_out)]
-    to_prev = push(ig_buf.at[0], nxt, {"section": lax.rem(sec + nsec - 1, nsec)})
-
     for c in range(2, len(chunks)):
         shared[c] = gather_far(shared[c], slots[c])
     got(slices0)
     over0 = []
-    for c, (lo, w, conv) in enumerate(chunks):
+
+    def cross(c):
+        lo, w, conv = chunks[c]
         got(shared[c])
         block = quarter(0, lo, w)
         zown[0, :, :, lo : lo + w] = block
@@ -440,6 +425,27 @@
         over0.append(spread(zs0[c], zr0[c]))
         if c == 0:
             next(ring1, None)
+
+    cross(0)
+    back_halo.wait_recv()
+
+    @pl.when(q == nq - 1)
+    def _():
+        hal_r[...] = jnp.zeros((32, chans), BF)
+
+    total = btw[...].astype(F32) + acc[...] + tap1[16 : 16 + rows] + tap2[32 : 32 + rows]
+    ig_buf[0, 0 : rows - 32] = total[0 : rows - 32].astype(BF)
+    ig_buf[0, rows - 32 : rows] = (total[rows - 32 :] + hal_r[...].astype(F32)).astype(BF)
+    def write(i, src, dst):
+        copy = pltpu.make_async_copy(src, dst, osem.at[i])
+        copy.start()
+        return copy
+
+    writes = [write(0, ig_buf, ig_out)]
+    to_prev = push(ig_buf.at[0], nxt, {"section": lax.rem(sec + nsec - 1, nsec)})
+
+    for c in range(1, len(chunks)):
+        cross(c)
     for _ in range(nz // 2 - 3):
         next(ring1, None)
 

time: 71 us -> 71 us (level)
  no operation moved by 1% of the time
where the time goes in v5:
time: 71 us; the launch traced here: 70.9 us
  Pallas kernels  70.2 us (99%)
    pallas_call x1, Pallas kernels, body(): pl.pallas_call(functools.partial(kernel, nz, nsec, chunks), out_shape=sha...  68.3 us
    pallas_call x1, Pallas kernels, body(): pl.pallas_call(hand_over, out_shape=shapes, in_specs=[any_] * 4, out_spec...  1.92 us

profile of v5, /device:TPU:14, one launch (start us, length us, event | category | flops | bytes accessed | tf_op | source)
XLA Modules:
  0.0 70.9 jit_solution(7276326568635782892)
XLA Ops:
  0.6 68.3 %shard_map.102 = (bf16[1,128,1024]{2,1,0:T(8,128)(2,1)}, bf16[1,128,1024]{2,1,0:T(8,128)(2,1)}, f32[1,32,2,1024]{3,2,1,0:T(2,128)}, f32[1,2,3,2,16,32]{5,4,3,2,1,0:T(8,128)}) custom-call(bf16[1,128,1024]{2,1,0:T(8,128)(2,1)} %refs_0_.1, bf16[1,128,1024]{2,1,0:T(8,128)(2,1)} %refs_1_.1, bf16[6,512,64]{2,1,0:T(8,128)(2,1)} %bitcast.8, ...), custom_call_target="tpu_custom_call" | custom-call | tf_op jit(solution)/shard_map/pallas_call | solution.py:559
  68.9 1.9 %shard_map.103 = (bf16[1,128,1024]{2,1,0:T(8,128)(2,1)}, bf16[1,128,1024]{2,1,0:T(8,128)(2,1)}, f32[1,32,2,1024]{3,2,1,0:T(2,128)}, f32[1,2,3,2,16,32]{5,4,3,2,1,0:T(8,128)}) custom-call(bf16[1,128,1024]{2,1,0:T(8,128)(2,1)} %get-tuple-element.8.refs_0_, bf16[1,128,1024]{2,1,0:T(8,128)(2,1)} %get-tuple-element.9.refs_1_, ...), custom_call_target="tpu_custom_call" | custom-call | tf_op jit(solution)/shard_map/pallas_call | solution.py:569
